TPU v7x, 512 devices: a whole 4x4x16 slice. The times are simulated.
512 devices in a mesh: dp: 32 (over z, x_hi), lon: 16 (over y, x_lo, core).
Axes of the slice: x: 4 (x_hi: 2, x_lo: 2; x = x_hi * 2 + x_lo), y: 4, z: 16, core: 2. Of those that a mesh axis runs over, the one named last changes fastest.
Arguments:
- fields: bfloat16 [32, 128, 48, 768], P('dp', 'lon'), may hold values from -6 to 6
- cotangent: bfloat16 [32, 128, 48, 768], P('dp', 'lon'), may hold values from -6 to 6
- first_weight: bfloat16 [2, 8, 96, 96], replicated, may hold values from -0.4375 to 0.4375
- second_weight: bfloat16 [2, 8, 96, 96], replicated, may hold values from -0.4375 to 0.4375
Outputs:
- layer_out: bfloat16 [32, 128, 48, 768], P('dp', 'lon')
- field_grad: bfloat16 [32, 128, 48, 768], P('dp', 'lon')
- first_grad: float32 [2, 8, 96, 96], replicated
- second_grad: float32 [2, 8, 96, 96], replicated
All inputs are finite; a program needn't handle non-finite values.
Results may differ from a plain program's by a relative error of at most 0.015.
Values may be sent and summed in bfloat16 or wider, within the bound.
A program may use at most 64 MiB of HBM per device.

v0:
```python
import math
import jax
import jax.numpy as jnp
from jax import lax
from jax.sharding import PartitionSpec as P

COEF = 0.7978845608028654
CUBIC = 0.044715


def gelu_value(inner):
    hyper = jnp.tanh(COEF * (inner + CUBIC * inner * inner * inner))
    return 0.5 * inner * (1.0 + hyper)


def gelu_slope(inner):
    hyper = jnp.tanh(COEF * (inner + CUBIC * inner * inner * inner))
    return 0.5 * (1.0 + hyper) + 0.5 * inner * (1.0 - hyper * hyper) * COEF * (
        1.0 + 3.0 * CUBIC * inner * inner
    )


def make_basis(length, count):
    cell_idx = jnp.arange(length, dtype=jnp.int32)
    mode_idx = jnp.arange(count, dtype=jnp.int32)
    product = cell_idx[:, None] * mode_idx[None, :] % length
    angle = product.astype(jnp.float32) * jnp.float32(2.0 * math.pi / length)
    return jnp.stack([jnp.cos(angle), -jnp.sin(angle)], axis=-1).astype(jnp.bfloat16)


def lat_apply(spec, table, lat_scale):
    return (
        jnp.einsum("kphc,phqj->kqjc", spec, table, preferred_element_type=jnp.float32) * lat_scale
    ).astype(jnp.bfloat16)


def forward_weight(weight):
    return jnp.stack([jnp.stack([weight[0], weight[1]]), jnp.stack([-weight[1], weight[0]])])


def adjoint_weight(weight):
    return jnp.stack([jnp.stack([weight[0], -weight[1]]), jnp.stack([weight[1], weight[0]])])


def block_product(spec, stacked):
    return jnp.einsum("kphbi,pqbij->kqhbj", spec, stacked, preferred_element_type=jnp.float32)


def block_adjoint(spec, stacked):
    return jnp.einsum("kphbj,pqbij->kqhbi", spec, stacked, preferred_element_type=jnp.float32)


def block_outer(left, right):
    pairs = jnp.einsum("kphbi,kqhbj->pqbij", left, right, preferred_element_type=jnp.float32)
    return jnp.stack([pairs[0, 0] + pairs[1, 1], pairs[0, 1] - pairs[1, 0]])


def on_device(fields, cotangent, first_weight, second_weight):
    cell_rows = fields[0]
    cot_rows = cotangent[0]
    lat_rows = cell_rows.shape[1]
    channels = cell_rows.shape[2]
    groups = first_weight.shape[1]
    group_width = first_weight.shape[2]
    lon_count = lax.axis_size("lon")
    total_cells = cell_rows.shape[0] * lon_count
    dft_basis = make_basis(total_cells, total_cells // 2)
    lat_basis = make_basis(lat_rows, lat_rows)
    cos_tab = lat_basis[:, :, 0]
    sin_tab = lat_basis[:, :, 1]
    lat_fwd_table = jnp.stack(
        [jnp.stack([cos_tab, sin_tab], axis=1), jnp.stack([-sin_tab, cos_tab], axis=1)], axis=0
    )
    lat_inv_table = jnp.stack(
        [jnp.stack([cos_tab.T, -sin_tab.T], axis=1), jnp.stack([sin_tab.T, cos_tab.T], axis=1)],
        axis=0,
    )
    norm_scale = 1.0 / math.sqrt(total_cells)
    lat_scale = 1.0 / math.sqrt(lat_rows)
    local_modes = cell_rows.shape[0] // 2
    mode_idx = lax.axis_index("lon") * local_modes + jnp.arange(local_modes, dtype=jnp.int32)
    mode_weight = jnp.where(mode_idx == 0, 1.0, 2.0).astype(jnp.bfloat16)[:, None, None, None]
    first_fwd = forward_weight(first_weight)
    second_fwd = forward_weight(second_weight)
    first_adj = adjoint_weight(first_weight)
    second_adj = adjoint_weight(second_weight)

    def local_dft(all_lines):
        return (
            jnp.einsum("whc,wkp->kphc", all_lines, dft_basis, preferred_element_type=jnp.float32)
            * norm_scale
        ).astype(jnp.bfloat16)

    def local_idft(all_modes):
        return (
            jnp.einsum("kphc,wkp->whc", all_modes, dft_basis, preferred_element_type=jnp.float32)
            * norm_scale
        ).astype(jnp.bfloat16)

    def lines_to_modes(all_lines):
        return lax.all_to_all(local_dft(all_lines), "lon", split_axis=0, concat_axis=3, tiled=True)

    def modes_to_lines(all_modes):
        return lax.all_to_all(local_idft(all_modes), "lon", split_axis=0, concat_axis=2, tiled=True)

    def to_spectrum(grid_rows):
        return lines_to_modes(
            lax.all_to_all(grid_rows, "lon", split_axis=2, concat_axis=0, tiled=True)
        )

    def to_cells(spec_rows):
        return modes_to_lines(
            lax.all_to_all(spec_rows, "lon", split_axis=3, concat_axis=0, tiled=True)
        )

    def split_groups(spec_rows):
        return spec_rows.reshape(local_modes, 2, lat_rows, groups, group_width)

    def join_groups(spec_rows):
        return spec_rows.astype(jnp.bfloat16).reshape(local_modes, 2, lat_rows, channels)

    lon_spec = to_spectrum(cell_rows)
    spectrum = split_groups(lat_apply(lon_spec, lat_fwd_table, lat_scale))
    inner = block_product(spectrum, first_fwd)
    act = gelu_value(inner).astype(jnp.bfloat16)
    mixed = join_groups(block_product(act, second_fwd)) * mode_weight
    mixed_lon = lat_apply(mixed, lat_inv_table, lat_scale)
    wave = to_cells(mixed_lon)
    dual_lon = to_spectrum(cot_rows)
    dual = split_groups(lat_apply(dual_lon, lat_fwd_table, lat_scale) * mode_weight)
    back = block_adjoint(dual, second_adj)
    pre = (back * gelu_slope(inner)).astype(jnp.bfloat16)
    back_spec = join_groups(block_adjoint(pre, first_adj))
    back_lon = lat_apply(back_spec, lat_inv_table, lat_scale)
    pull = to_cells(back_lon)
    layer_out = (cell_rows.astype(jnp.float32) + wave.astype(jnp.float32)).astype(jnp.bfloat16)
    field_grad = (cot_rows.astype(jnp.float32) + pull.astype(jnp.float32)).astype(jnp.bfloat16)
    sample_count = lax.axis_size("dp")
    second_term = block_outer(act, dual) / sample_count
    first_term = block_outer(spectrum, pre) / sample_count
    first_grad, second_grad = lax.psum((first_term, second_term), ("dp", "lon"))
    return (layer_out[None], field_grad[None], first_grad, second_grad)


def solution(mesh):
    placed = (P("dp", "lon", None, None), P("dp", "lon", None, None), P(), P())
    return jax.shard_map(
        on_device,
        mesh=mesh,
        in_specs=placed,
        out_specs=(P("dp", "lon", None, None), P("dp", "lon", None, None), P(), P()),
        check_vma=False,
    )
```

profile of v0, /device:TPU:1, one launch (start us, length us, event | category | flops | bytes accessed | tf_op | source)
XLA Modules:
  0.0 643.6 jit_solution(1187848861176454927)
XLA Ops:
  9.3 3.1 reshape.309
  12.4 11.0 %all-to-all-start = ((bf16[16,2,9216]{2,1,0:T(2,128)(2,1)}), bf16[16,2,9216]{2,1,0:T(2,128)(2,1)}, u32[]{:S(2)}, u32[]{:S(2)}) async-start(bf16[16,2,9216]{2,1,0:T(2,128)(2,1)} %reshape.309), calls=%async_computation | async-start | bytes 1179648 | tf_op jit(solution)/shard_map/all_to_all | solution.py:108
  24.6 3.1 reshape.317
  30.0 4.0 all-to-all-done
  34.1 5.2 all-to-all-start.4
  40.8 2.4 reshape.310
  47.2 3.1 reshape.311
  50.3 6.4 %all-to-all-start.1 = ((bf16[16,2,9216]{2,1,0:T(2,128)(2,1)}), bf16[16,2,9216]{2,1,0:T(2,128)(2,1)}, u32[]{:S(2)}, u32[]{:S(2)}) async-start(bf16[16,2,9216]{2,1,0:T(2,128)(2,1)} %reshape.311), calls=%async_computation.1 | async-start | bytes 1179648 | tf_op jit(solution)/shard_map/all_to_all | solution.py:101
  59.0 2.4 reshape.318
  65.4 3.1 reshape.319
  68.5 5.9 all-to-all-start.5
  77.1 2.4 reshape.312
  85.0 2.4 reshape.320
  89.7 2.9 reshape.288
  101.3 3.1 reshape.321
  104.4 4.5 all-to-all-start.6
  113.5 2.2 copy.132
  115.7 4.1 reshape.313
  121.4 5.8 all-to-all-start.2
  135.6 3.1 reshape.323
  138.7 5.7 all-to-all-start.7
  144.4 2.4 reshape.314
  151.4 3.1 reshape.315
  154.5 451.1 %all-reduce.3.cloned.1.call-done = (f32[2,8,96,96]{2,3,1,0:T(8,128)}, f32[2,8,96,96]{2,3,1,0:T(8,128)}) async-done(((f32[2,8,96,96]{2,3,1,0:T(8,128)}, f32[2,8,96,96]{2,3,1,0:T(8,128)}), (f32[2,8,96,96]{2,3,1,0:T(8,128)}, f32[2,8,96,96]{2,3,1,0:T(8,128)})) %all-reduce.3.cloned.1.call-update) | async-done | bytes 1179664 | tf_op jit(solution)/shard_map/psum | solution.py:141
  605.7 2.4 copy.158
  609.2 7.4 %all-to-all-start.3 = ((bf16[16,2,9216]{2,1,0:T(2,128)(2,1)}), bf16[16,2,9216]{2,1,0:T(2,128)(2,1)}, u32[]{:S(2)}, u32[]{:S(2)}) async-start(bf16[16,2,9216]{2,1,0:T(2,128)(2,1)} %reshape.315), calls=%async_computation.3 | async-start | bytes 1179648 | tf_op jit(solution)/shard_map/all_to_all | solution.py:104
  616.6 2.4 reshape.324
  621.2 2.2 reshape.269
  623.5 2.3 add_convert_fusion
  627.1 2.4 reshape.316
  631.7 2.2 reshape.268
  634.0 2.3 add_convert_fusion.1
  (139 shorter events, 61.8 us)
Async XLA Ops:
  12.3 11.0 %copy-start = (bf16[1,8,48,768]{3,2,1,0:T(8,128)(2,1)S(1)}, bf16[1,8,48,768]{3,2,1,0:T(8,128)(2,1)}, u32[]{:S(2)}) copy-start(bf16[1,8,48,768]{3,2,1,0:T(8,128)(2,1)} %param.5) | copy-start | bytes 1769476
  12.4 21.7 %all-to-all-start = ((bf16[16,2,9216]{2,1,0:T(2,128)(2,1)}), bf16[16,2,9216]{2,1,0:T(2,128)(2,1)}, u32[]{:S(2)}, u32[]{:S(2)}) async-start(bf16[16,2,9216]{2,1,0:T(2,128)(2,1)} %reshape.309), calls=%async_computation | async-start | bytes 1179648 | tf_op jit(solution)/shard_map/all_to_all | solution.py:108
  24.6 15.4 %copy-start.21 = (bf16[2,8,96,96]{3,2,1,0:T(8,128)(2,1)S(1)}, bf16[2,8,96,96]{3,2,1,0:T(8,128)(2,1)}, u32[]{:S(2)}) copy-start(bf16[2,8,96,96]{3,2,1,0:T(8,128)(2,1)} %param.6) | copy-start | bytes 884740
  34.1 16.2 %all-to-all-start.4 = ((bf16[16,2,9216]{2,1,0:T(2,128)(2,1)}), bf16[16,2,9216]{2,1,0:T(2,128)(2,1)}, u32[]{:S(2)}, u32[]{:S(2)}) async-start(bf16[16,2,9216]{2,1,0:T(2,128)(2,1)} %reshape.317), calls=%async_computation.4 | async-start | bytes 1179648 | tf_op jit(solution)/shard_map/all_to_all | solution.py:108
  47.2 9.6 %copy-start.29 = (bf16[48,1,48]{2,0,1:T(8,128)(2,1)S(1)}, bf16[48,1,48]{2,0,1:T(8,128)(2,1)}, u32[]{:S(2)}) copy-start(bf16[48,1,48]{2,0,1:T(8,128)(2,1)} %get-tuple-element.48) | copy-start | bytes 13828
  47.2 9.6 %copy-start.30 = (bf16[48,1,48]{2,0,1:T(8,128)(2,1)S(1)}, bf16[48,1,48]{2,0,1:T(8,128)(2,1)}, u32[]{:S(2)}) copy-start(bf16[48,1,48]{2,0,1:T(8,128)(2,1)} %get-tuple-element.49) | copy-start | bytes 13828
  47.2 9.6 %copy-start.31 = (bf16[48,1,48]{2,0,1:T(8,128)(2,1)S(1)}, bf16[48,1,48]{2,0,1:T(8,128)(2,1)}, u32[]{:S(2)}) copy-start(bf16[48,1,48]{2,0,1:T(8,128)(2,1)} %fusion.91) | copy-start | bytes 13828
  47.2 10.2 %copy-start.22 = (bf16[2,8,96,96]{3,2,1,0:T(8,128)(2,1)S(1)}, bf16[2,8,96,96]{3,2,1,0:T(8,128)(2,1)}, u32[]{:S(2)}) copy-start(bf16[2,8,96,96]{3,2,1,0:T(8,128)(2,1)} %param.7) | copy-start | bytes 884740
  50.3 18.2 %all-to-all-start.1 = ((bf16[16,2,9216]{2,1,0:T(2,128)(2,1)}), bf16[16,2,9216]{2,1,0:T(2,128)(2,1)}, u32[]{:S(2)}, u32[]{:S(2)}) async-start(bf16[16,2,9216]{2,1,0:T(2,128)(2,1)} %reshape.311), calls=%async_computation.1 | async-start | bytes 1179648 | tf_op jit(solution)/shard_map/all_to_all | solution.py:101
  65.4 9.5 %copy-start.8 = (bf16[1,8,96,96]{3,2,0,1:T(8,128)(2,1)S(1)}, bf16[1,8,96,96]{3,2,0,1:T(8,128)(2,1)}, u32[]{:S(2)}) copy-start(bf16[1,8,96,96]{3,2,0,1:T(8,128)(2,1)} %get-tuple-element.26) | copy-start | bytes 442372
  65.4 9.5 %copy-start.9 = (bf16[1,8,96,96]{3,2,0,1:T(8,128)(2,1)S(1)}, bf16[1,8,96,96]{3,2,0,1:T(8,128)(2,1)}, u32[]{:S(2)}) copy-start(bf16[1,8,96,96]{3,2,0,1:T(8,128)(2,1)} %get-tuple-element.27) | copy-start | bytes 442372
  65.4 9.5 %copy-start.10 = (bf16[1,8,96,96]{3,2,0,1:T(8,128)(2,1)S(1)}, bf16[1,8,96,96]{3,2,0,1:T(8,128)(2,1)}, u32[]{:S(2)}) copy-start(bf16[1,8,96,96]{3,2,0,1:T(8,128)(2,1)} %get-tuple-element.28) | copy-start | bytes 442372
  68.5 7.5 %copy-start.11 = (bf16[1,8,96,96]{3,2,0,1:T(8,128)(2,1)S(1)}, bf16[1,8,96,96]{3,2,0,1:T(8,128)(2,1)}, u32[]{:S(2)}) copy-start(bf16[1,8,96,96]{3,2,0,1:T(8,128)(2,1)} %get-tuple-element.31) | copy-start | bytes 442372
  68.5 7.5 %copy-start.12 = (bf16[1,8,96,96]{3,2,0,1:T(8,128)(2,1)S(1)}, bf16[1,8,96,96]{3,2,0,1:T(8,128)(2,1)}, u32[]{:S(2)}) copy-start(bf16[1,8,96,96]{3,2,0,1:T(8,128)(2,1)} %get-tuple-element.32) | copy-start | bytes 442372
  68.5 7.5 %copy-start.13 = (bf16[1,8,96,96]{3,2,0,1:T(8,128)(2,1)S(1)}, bf16[1,8,96,96]{3,2,0,1:T(8,128)(2,1)}, u32[]{:S(2)}) copy-start(bf16[1,8,96,96]{3,2,0,1:T(8,128)(2,1)} %get-tuple-element.33) | copy-start | bytes 442372
  68.5 16.5 %all-to-all-start.5 = ((bf16[16,2,9216]{2,1,0:T(2,128)(2,1)}), bf16[16,2,9216]{2,1,0:T(2,128)(2,1)}, u32[]{:S(2)}, u32[]{:S(2)}) async-start(bf16[16,2,9216]{2,1,0:T(2,128)(2,1)} %reshape.319), calls=%async_computation.5 | async-start | bytes 1179648 | tf_op jit(solution)/shard_map/all_to_all | solution.py:101
  80.6 1.6 copy-start.25
  80.6 1.6 copy-start.27
  89.7 2.9 copy-start.26
  89.7 2.9 copy-start.28
  89.7 2.9 copy-start.32
  94.8 1.7 copy-start.7
  94.8 1.7 copy-start.19
  94.8 1.6 copy-start.20
  96.5 1.3 copy-start.18
  101.3 7.6 %copy-start.3 = (bf16[2,8,96,96]{3,2,0,1:T(8,128)(2,1)S(1)}, bf16[2,8,96,96]{3,2,0,1:T(8,128)(2,1)}, u32[]{:S(2)}) copy-start(bf16[2,8,96,96]{3,2,0,1:T(8,128)(2,1)} %copy-done.2) | copy-start | bytes 884740
  104.4 17.0 %all-to-all-start.6 = ((bf16[16,2,9216]{2,1,0:T(2,128)(2,1)}), bf16[16,2,9216]{2,1,0:T(2,128)(2,1)S(1)}, u32[]{:S(2)}, u32[]{:S(2)}) async-start(bf16[16,2,9216]{2,1,0:T(2,128)(2,1)} %reshape.321), calls=%async_computation.6 | async-start | bytes 1179648 | tf_op jit(solution)/shard_map/all_to_all | solution.py:113
  121.4 17.3 %all-to-all-start.2 = ((bf16[16,2,9216]{2,1,0:T(2,128)(2,1)}), bf16[16,2,9216]{2,1,0:T(2,128)(2,1)}, u32[]{:S(2)}, u32[]{:S(2)}) async-start(bf16[16,2,9216]{2,1,0:T(2,128)(2,1)} %reshape.313), calls=%async_computation.2 | async-start | bytes 1179648 | tf_op jit(solution)/shard_map/all_to_all | solution.py:113
  127.2 478.5 %all-reduce.3.cloned.1.call-start = ((), (), s32[]{:S(2)}) async-start(), calls=%async_computation.8 | async-start | bytes 3145728 | tf_op jit(solution)/shard_map/psum | solution.py:141
  138.7 470.5 %all-to-all-start.7 = ((bf16[16,2,9216]{2,1,0:T(2,128)(2,1)}), bf16[16,2,9216]{2,1,0:T(2,128)(2,1)}, u32[]{:S(2)}, u32[]{:S(2)}) async-start(bf16[16,2,9216]{2,1,0:T(2,128)(2,1)} %reshape.323), calls=%async_computation.7 | async-start | bytes 1179648 | tf_op jit(solution)/shard_map/all_to_all | solution.py:104
  605.7 2.4 copy-start.4
  609.2 17.9 %all-to-all-start.3 = ((bf16[16,2,9216]{2,1,0:T(2,128)(2,1)}), bf16[16,2,9216]{2,1,0:T(2,128)(2,1)}, u32[]{:S(2)}, u32[]{:S(2)}) async-start(bf16[16,2,9216]{2,1,0:T(2,128)(2,1)} %reshape.315), calls=%async_computation.3 | async-start | bytes 1179648 | tf_op jit(solution)/shard_map/all_to_all | solution.py:104
  (10 other events, 11.0 us)
Sparse Core Ops, SparseCore 0:
  133.9 471.6 all-reduce.2
where the time goes:
time: 652 us; the launch traced here: 644 us
  waiting for transfers between devices  458 us (70%)
  local copies, waits for them, and re-layouts  88.6 us (14%)
  starting transfers between devices  52 us (8%)
  other arithmetic  17.4 us (3%)
  between operations  15.2 us (2%)
  matrix products  12.2 us (2%)
    psum x1, waiting for transfers between devices, on_device(): first_grad, second_grad = lax.psum((first_term, second_term), ('dp', 'lon'))  451 us
    unnamed x90, local copies, waits for them, and re-layouts  52.7 us
    all_to_all x2, starting transfers between devices, to_spectrum(): lax.all_to_all(grid_rows, 'lon', split_axis=2, concat_axis=0, tiled=True)  16.1 us
    all_to_all x2, starting transfers between devices, modes_to_lines(): lax.all_to_all(local_idft(all_modes), 'lon', split_axis=0, concat_axis=2,...  13.2 us
  transfers between devices with their start and end apart: 9, of which 4 were waited for; matrix products, arithmetic and copies ran while one was open for 13% of the time, Pallas kernels for 0%

commit v1 on v0

--- a/solution.py
+++ b/solution.py
@@ -98,7 +98,15 @@
         ).astype(jnp.bfloat16)
 
     def lines_to_modes(all_lines):
-        return lax.all_to_all(local_dft(all_lines), "lon", split_axis=0, concat_axis=3, tiled=True)
+        return jnp.concatenate(
+            lax.all_to_all(
+                jnp.stack(jnp.split(local_dft(all_lines), lax.axis_size("lon"), axis=0)),
+                "lon",
+                0,
+                0,
+            ),
+            axis=3,
+        )
 
     def modes_to_lines(all_modes):
         return lax.all_to_all(local_idft(all_modes), "lon", split_axis=0, concat_axis=2, tiled=True)

time: 652 us -> 762 us (1.17)
  local copies, waits for them, and re-layouts: 88.6 us -> 204 us
    another operation x0 -> x36, local copies, waits for them, and re-layouts: none -> 92.1 us  [lines_to_modes(): jnp.stack(jnp.split(local_dft(all_lines), lax.axis_size('lon'), axis=0))]
    unnamed x90 -> x162, local copies, waits for them, and re-layouts: 52.7 us -> 79.9 us
    all_to_all x4 -> x0, local copies, waits for them, and re-layouts: 7.68 us -> none  [lines_to_modes(): lax.all_to_all(local_dft(all_lines), 'lon', split_axis=0, concat_axis=3,...]
  transfers between devices with their start and end apart: 9 -> 9, of which waited for: 4 -> 4; matrix products, arithmetic and copies ran while one was open for 13% -> 26% of each run, Pallas kernels for 0% -> 0%
where the time goes in v1:
time: 762 us; the launch traced here: 755 us
  waiting for transfers between devices  456 us (60%)
  local copies, waits for them, and re-layouts  204 us (27%)
  starting transfers between devices  52.6 us (7%)
  other arithmetic  15.7 us (2%)
  between operations  15.4 us (2%)
  matrix products  12.2 us (2%)
    psum x1, waiting for transfers between devices, on_device(): first_grad, second_grad = lax.psum((first_term, second_term), ('dp', 'lon'))  451 us
    another operation x36, local copies, waits for them, and re-layouts, lines_to_modes(): jnp.stack(jnp.split(local_dft(all_lines), lax.axis_size('lon'), axis=0))  92.1 us
    unnamed x162, local copies, waits for them, and re-layouts  79.9 us
    all_to_all x2, starting transfers between devices, to_spectrum(): lax.all_to_all(grid_rows, 'lon', split_axis=2, concat_axis=0, tiled=True)  16.5 us
  transfers between devices with their start and end apart: 9, of which 4 were waited for; matrix products, arithmetic and copies ran while one was open for 26% of the time, Pallas kernels for 0%

profile of v1, /device:TPU:1, one launch (start us, length us, event | category | flops | bytes accessed | tf_op | source)
XLA Modules:
  0.0 755.3 jit_solution(17666405755317642792)
XLA Ops:
  9.3 3.1 reshape.333
  12.4 11.0 %all-to-all-start.4 = ((bf16[16,2,9216]{2,1,0:T(2,128)(2,1)}), bf16[16,2,9216]{2,1,0:T(2,128)(2,1)}, u32[]{:S(2)}, u32[]{:S(2)}) async-start(bf16[16,2,9216]{2,1,0:T(2,128)(2,1)} %reshape.333), calls=%async_computation.4 | async-start | bytes 1179648 | tf_op jit(solution)/shard_map/all_to_all | solution.py:116
  25.1 3.1 reshape.325
  34.1 5.5 all-to-all-start
  44.6 7.9 %slice_bitcast_fusion = (bf16[1,4,2,48,48]{1,4,3,2,0:T(8,128)(2,1)S(1)}, bf16[1,4,2,48,48]{1,4,3,2,0:T(8,128)(2,1)S(1)}, bf16[1,4,2,48,48]{1,4,3,2,0:T(8,128)(2,...) fusion(bf16[64,2,48,48]{0,3,2,1:T(8,128)(2,1)S(1)} %multiply_co, ...), kind=kLoop, calls=%fused_computation.48 | loop fusion | bytes 1179648 | tf_op jit(solution)/shard_map/stack | solution.py:103
  52.5 2.7 copy.149
  62.0 2.7 copy.152
  67.3 2.7 copy.154
  75.3 2.7 copy.157
  80.6 2.7 copy.159
  85.9 2.7 copy.161
  103.1 4.1 reshape.335
  107.3 6.3 all-to-all-start.5
  118.6 7.9 %slice_bitcast_fusion.16 = (bf16[1,4,2,48,48]{1,4,3,2,0:T(8,128)(2,1)S(1)}, bf16[1,4,2,48,48]{1,4,3,2,0:T(8,128)(2,1)S(1)}, bf16[1,4,2,48,48]{1,4,3,2,0:T(8,128)...) fusion(bf16[64,2,48,48]{0,3,2,1:T(8,128)(2,1)S(1)} %multiply_co, ...), kind=kLoop, calls=%fused_computation.64 | loop fusion | bytes 1179648 | tf_op jit(solution)/shard_map/stack | solution.py:103
  126.5 2.7 copy.120
  136.0 2.7 copy.123
  141.3 2.7 copy.125
  152.0 2.7 copy.129
  154.7 2.7 copy.130
  157.3 2.7 copy.131
  160.0 2.7 copy.132
  177.2 4.4 reshape.327
  181.6 5.9 all-to-all-start.1
  212.6 3.1 reshape.337
  215.7 5.0 all-to-all-start.6
  227.5 4.1 reshape.329
  233.1 5.7 all-to-all-start.2
  247.3 3.1 reshape.339
  250.4 5.7 all-to-all-start.7
  263.2 3.1 reshape.331
  266.2 451.0 %all-reduce.3.cloned.1.call-done = (f32[2,8,96,96]{2,3,1,0:T(8,128)}, f32[2,8,96,96]{2,3,1,0:T(8,128)}) async-done(((f32[2,8,96,96]{2,3,1,0:T(8,128)}, f32[2,8,96,96]{2,3,1,0:T(8,128)}), (f32[2,8,96,96]{2,3,1,0:T(8,128)}, f32[2,8,96,96]{2,3,1,0:T(8,128)})) %all-reduce.3.cloned.1.call-update) | async-done | bytes 1179664 | tf_op jit(solution)/shard_map/psum | solution.py:149
  720.8 7.5 all-to-all-start.3
  (245 shorter events, 157.7 us)
Async XLA Ops:
  12.3 11.5 %copy-start.2 = (bf16[1,8,48,768]{3,2,1,0:T(8,128)(2,1)S(1)}, bf16[1,8,48,768]{3,2,1,0:T(8,128)(2,1)}, u32[]{:S(2)}) copy-start(bf16[1,8,48,768]{3,2,1,0:T(8,128)(2,1)} %param.4) | copy-start | bytes 1769476
  12.4 21.7 %all-to-all-start.4 = ((bf16[16,2,9216]{2,1,0:T(2,128)(2,1)}), bf16[16,2,9216]{2,1,0:T(2,128)(2,1)}, u32[]{:S(2)}, u32[]{:S(2)}) async-start(bf16[16,2,9216]{2,1,0:T(2,128)(2,1)} %reshape.333), calls=%async_computation.4 | async-start | bytes 1179648 | tf_op jit(solution)/shard_map/all_to_all | solution.py:116
  29.8 14.3 %copy-start.16 = (bf16[128,64,1]{0,1,2:T(8,128)(2,1)}, bf16[128,64,1]{0,1,2:T(8,128)(2,1)S(1)}, u32[]{:S(2)}) copy-start(bf16[128,64,1]{0,1,2:T(8,128)(2,1)S(1)} %get-tuple-element.77) | copy-start | bytes 49156
  34.1 73.2 %all-to-all-start = ((bf16[16,2,9216]{2,1,0:T(2,128)(2,1)}), bf16[16,2,9216]{2,1,0:T(2,128)(2,1)}, u32[]{:S(2)}, u32[]{:S(2)}) async-start(bf16[16,2,9216]{2,1,0:T(2,128)(2,1)} %reshape.325), calls=%async_computation | async-start | bytes 1179648 | tf_op jit(solution)/shard_map/all_to_all | solution.py:116
  90.0 7.3 copy-start.37
  90.8 7.2 copy-start.35
  90.8 7.8 %copy-start.33 = (bf16[1,4,2,48,48]{4,3,2,1,0:T(8,128)(2,1)S(1)}, bf16[1,4,2,48,48]{4,3,2,1,0:T(8,128)(2,1)}, u32[]{:S(2)}) copy-start(bf16[1,4,2,48,48]{4,3,2,1,0:T(8,128)(2,1)} %copy.158) | copy-start | bytes 110596
  90.8 8.5 %copy-start.31 = (bf16[1,4,2,48,48]{4,3,2,1,0:T(8,128)(2,1)S(1)}, bf16[1,4,2,48,48]{4,3,2,1,0:T(8,128)(2,1)}, u32[]{:S(2)}) copy-start(bf16[1,4,2,48,48]{4,3,2,1,0:T(8,128)(2,1)} %copy.159) | copy-start | bytes 110596
  90.8 9.1 %copy-start.29 = (bf16[1,4,2,48,48]{4,3,2,1,0:T(8,128)(2,1)S(1)}, bf16[1,4,2,48,48]{4,3,2,1,0:T(8,128)(2,1)}, u32[]{:S(2)}) copy-start(bf16[1,4,2,48,48]{4,3,2,1,0:T(8,128)(2,1)} %copy.160) | copy-start | bytes 110596
  90.8 9.7 %copy-start.27 = (bf16[1,4,2,48,48]{4,3,2,1,0:T(8,128)(2,1)S(1)}, bf16[1,4,2,48,48]{4,3,2,1,0:T(8,128)(2,1)}, u32[]{:S(2)}) copy-start(bf16[1,4,2,48,48]{4,3,2,1,0:T(8,128)(2,1)} %copy.161) | copy-start | bytes 110596
  90.8 10.4 %copy-start.25 = (bf16[1,4,2,48,48]{4,3,2,1,0:T(8,128)(2,1)S(1)}, bf16[1,4,2,48,48]{4,3,2,1,0:T(8,128)(2,1)}, u32[]{:S(2)}) copy-start(bf16[1,4,2,48,48]{4,3,2,1,0:T(8,128)(2,1)} %copy.162) | copy-start | bytes 110596
  107.3 74.3 %all-to-all-start.5 = ((bf16[16,2,9216]{2,1,0:T(2,128)(2,1)}), bf16[16,2,9216]{2,1,0:T(2,128)(2,1)}, u32[]{:S(2)}, u32[]{:S(2)}) async-start(bf16[16,2,9216]{2,1,0:T(2,128)(2,1)} %reshape.335), calls=%async_computation.5 | async-start | bytes 1179648 | tf_op jit(solution)/shard_map/all_to_all | solution.py:102
  164.1 7.3 copy-start.38
  164.9 7.2 copy-start.36
  164.9 7.8 %copy-start.34 = (bf16[1,4,2,48,48]{4,3,2,1,0:T(8,128)(2,1)S(1)}, bf16[1,4,2,48,48]{4,3,2,1,0:T(8,128)(2,1)}, u32[]{:S(2)}) copy-start(bf16[1,4,2,48,48]{4,3,2,1,0:T(8,128)(2,1)} %copy.129) | copy-start | bytes 110596
  164.9 8.5 %copy-start.32 = (bf16[1,4,2,48,48]{4,3,2,1,0:T(8,128)(2,1)S(1)}, bf16[1,4,2,48,48]{4,3,2,1,0:T(8,128)(2,1)}, u32[]{:S(2)}) copy-start(bf16[1,4,2,48,48]{4,3,2,1,0:T(8,128)(2,1)} %copy.130) | copy-start | bytes 110596
  164.9 9.1 %copy-start.30 = (bf16[1,4,2,48,48]{4,3,2,1,0:T(8,128)(2,1)S(1)}, bf16[1,4,2,48,48]{4,3,2,1,0:T(8,128)(2,1)}, u32[]{:S(2)}) copy-start(bf16[1,4,2,48,48]{4,3,2,1,0:T(8,128)(2,1)} %copy.131) | copy-start | bytes 110596
  164.9 9.7 %copy-start.28 = (bf16[1,4,2,48,48]{4,3,2,1,0:T(8,128)(2,1)S(1)}, bf16[1,4,2,48,48]{4,3,2,1,0:T(8,128)(2,1)}, u32[]{:S(2)}) copy-start(bf16[1,4,2,48,48]{4,3,2,1,0:T(8,128)(2,1)} %copy.132) | copy-start | bytes 110596
  164.9 10.4 %copy-start.26 = (bf16[1,4,2,48,48]{4,3,2,1,0:T(8,128)(2,1)S(1)}, bf16[1,4,2,48,48]{4,3,2,1,0:T(8,128)(2,1)}, u32[]{:S(2)}) copy-start(bf16[1,4,2,48,48]{4,3,2,1,0:T(8,128)(2,1)} %copy.133) | copy-start | bytes 110596
  177.2 10.9 %copy-start.13 = (bf16[1,8,96,96]{3,2,0,1:T(8,128)(2,1)S(1)}, bf16[1,8,96,96]{3,2,0,1:T(8,128)(2,1)}, u32[]{:S(2)}) copy-start(bf16[1,8,96,96]{3,2,0,1:T(8,128)(2,1)} %get-tuple-element.58) | copy-start | bytes 442372
  177.2 10.9 %copy-start.14 = (bf16[1,8,96,96]{3,2,0,1:T(8,128)(2,1)S(1)}, bf16[1,8,96,96]{3,2,0,1:T(8,128)(2,1)}, u32[]{:S(2)}) copy-start(bf16[1,8,96,96]{3,2,0,1:T(8,128)(2,1)} %get-tuple-element.59) | copy-start | bytes 442372
  177.2 10.9 %copy-start.15 = (bf16[1,8,96,96]{3,2,0,1:T(8,128)(2,1)S(1)}, bf16[1,8,96,96]{3,2,0,1:T(8,128)(2,1)}, u32[]{:S(2)}) copy-start(bf16[1,8,96,96]{3,2,0,1:T(8,128)(2,1)} %get-tuple-element.60) | copy-start | bytes 442372
  181.6 7.5 copy-start.10
  181.6 7.5 copy-start.11
  181.6 7.5 copy-start.12
  181.6 16.5 %all-to-all-start.1 = ((bf16[16,2,9216]{2,1,0:T(2,128)(2,1)}), bf16[16,2,9216]{2,1,0:T(2,128)(2,1)}, u32[]{:S(2)}, u32[]{:S(2)}) async-start(bf16[16,2,9216]{2,1,0:T(2,128)(2,1)} %reshape.327), calls=%async_computation.1 | async-start | bytes 1179648 | tf_op jit(solution)/shard_map/all_to_all | solution.py:102
  212.6 8.0 %copy-start.4 = (bf16[2,8,96,96]{3,2,0,1:T(8,128)(2,1)S(1)}, bf16[2,8,96,96]{3,2,0,1:T(8,128)(2,1)}, u32[]{:S(2)}) copy-start(bf16[2,8,96,96]{3,2,0,1:T(8,128)(2,1)} %copy-done.3) | copy-start | bytes 884740
  215.7 17.4 %all-to-all-start.6 = ((bf16[16,2,9216]{2,1,0:T(2,128)(2,1)}), bf16[16,2,9216]{2,1,0:T(2,128)(2,1)S(1)}, u32[]{:S(2)}, u32[]{:S(2)}) async-start(bf16[16,2,9216]{2,1,0:T(2,128)(2,1)} %reshape.337), calls=%async_computation.6 | async-start | bytes 1179648 | tf_op jit(solution)/shard_map/all_to_all | solution.py:121
  233.1 17.3 %all-to-all-start.2 = ((bf16[16,2,9216]{2,1,0:T(2,128)(2,1)}), bf16[16,2,9216]{2,1,0:T(2,128)(2,1)}, u32[]{:S(2)}, u32[]{:S(2)}) async-start(bf16[16,2,9216]{2,1,0:T(2,128)(2,1)} %reshape.329), calls=%async_computation.2 | async-start | bytes 1179648 | tf_op jit(solution)/shard_map/all_to_all | solution.py:121
  238.8 478.5 %all-reduce.3.cloned.1.call-start = ((), (), s32[]{:S(2)}) async-start(), calls=%async_computation.8 | async-start | bytes 3145728 | tf_op jit(solution)/shard_map/psum | solution.py:149
  250.4 470.4 %all-to-all-start.7 = ((bf16[16,2,9216]{2,1,0:T(2,128)(2,1)}), bf16[16,2,9216]{2,1,0:T(2,128)(2,1)}, u32[]{:S(2)}, u32[]{:S(2)}) async-start(bf16[16,2,9216]{2,1,0:T(2,128)(2,1)} %reshape.339), calls=%async_computation.7 | async-start | bytes 1179648 | tf_op jit(solution)/shard_map/all_to_all | solution.py:112
  720.8 18.0 %all-to-all-start.3 = ((bf16[16,2,9216]{2,1,0:T(2,128)(2,1)}), bf16[16,2,9216]{2,1,0:T(2,128)(2,1)}, u32[]{:S(2)}, u32[]{:S(2)}) async-start(bf16[16,2,9216]{2,1,0:T(2,128)(2,1)} %reshape.331), calls=%async_computation.3 | async-start | bytes 1179648 | tf_op jit(solution)/shard_map/all_to_all | solution.py:112
  (31 other events, 89.5 us)
Sparse Core Ops, SparseCore 0:
  245.6 471.6 all-reduce.2
